TPU v7x, 32 devices: a whole 2x2x4 slice. The times are simulated.
32 devices in a mesh: groups: 2 (over x), seq: 16 (over z, y, core).
Axes of the slice: x: 2, y: 2, z: 4, core: 2. Of those that a mesh axis runs over, the one named last changes fastest.
Arguments:
- cache_keys: bfloat16 [131072, 1024], P(('groups', 'seq')), parts along dimension 0, may hold values from -48 to 48
- cache_values: bfloat16 [131072, 1024], P(('groups', 'seq')), parts along dimension 0, may hold values from -6 to 6
- sketch_matrix: float32 [1024, 160], replicated, may hold values from -6 to 6
- queries: bfloat16 [6, 8192], P('groups'), parts along dimension 0, may hold values from -2000 to 2000
- fresh_keys: bfloat16 [6, 1024], P('groups'), parts along dimension 0, may hold values from -20 to 20
- fresh_values: bfloat16 [6, 1024], P('groups'), parts along dimension 0, may hold values from -6 to 6
- chosen: int32 [6, 8, 256], P('groups'), parts along dimension 0, may hold values from 0 to 8191, as said below
- shard_counts: int32 [6, 8, 16], P('groups'), parts along dimension 0, may hold values from 0 to 48, as said below
- outliers: int32 [64], P('groups'), parts along dimension 0, may hold values from 0 to 8191, as said below
Outputs:
- attended: bfloat16 [6, 8192], P('groups', 'seq'), parts along dimension 0
- key_factor: float32 [131072, 160], P(('groups', 'seq')), parts along dimension 0
There are 2 independent parts, one for each index of `groups`. A program takes and returns all parts, laid end to end along the dimension named above; an argument that names none is the same for every part. Nothing has to cross between parts.
Inputs may be any that keep to these rules, and one draw needn't show every extreme that they name: Each list chosen[t, g] holds distinct span numbers in ascending order, none of them an outlier span; shard s holds spans s * 512 to (s+1) * 512 - 1. shard_counts[t, g, s] is the number of entries of chosen[t, g] on shard s; they sum to 256; the most is 48, reached in every list. `outliers`: distinct span numbers in ascending order; at most 4 on one shard, reached on some shard.
All inputs are finite; a program needn't handle non-finite values.
Results may differ from a plain program's by a relative error of at most 0.0228.
Values may be sent and summed in bfloat16 or wider, within the bound.
A program may use at most 128 MiB of HBM per device.

v0:
```python
import jax
import jax.numpy as jnp
from jax import lax
from jax.sharding import PartitionSpec as P

KVH = 8
HD = 128
QH = 64
SPAN = 8
OMOST = 4


def merged_2(x, axis, combine):
    everything = jax.tree.map(lambda part: lax.all_gather(part, axis), x)
    leading = jax.tree.map(lambda part: part[0], everything)

    def step(k, so_far):
        return combine(so_far, jax.tree.map(lambda part: part[k], everything))

    return lax.fori_loop(1, lax.axis_size(axis), step, leading)


def rotate(vectors, positions):
    half_width = vectors.shape[-1] // 2
    exponents = jnp.arange(half_width, dtype=jnp.float32) * (2.0 / vectors.shape[-1])
    inverse_freq = jnp.exp(-jnp.log(jnp.float32(500000.0)) * exponents)
    angles = positions.astype(jnp.float32)[..., None] * inverse_freq
    cosine = jnp.cos(angles)
    sine = jnp.sin(angles)
    first_half = vectors[..., :half_width]
    second_half = vectors[..., half_width:]
    return jnp.concatenate(
        [first_half * cosine - second_half * sine, second_half * cosine + first_half * sine],
        axis=-1,
    )


def make_basis(sketch):
    small_gram = jnp.dot(sketch.T, sketch, precision=lax.Precision.HIGHEST)
    lower = jnp.linalg.cholesky(small_gram)
    solved = lax.linalg.triangular_solve(lower, sketch.T, left_side=True, lower=True)
    return solved.T.astype(jnp.bfloat16)


def softmax_part(query_rows, key_rows, value_rows, is_live):
    score_scale = 1.0 / jnp.sqrt(jnp.float32(query_rows.shape[-1]))
    scores = (
        jnp.einsum(
            "...qd,...ld->...ql",
            query_rows,
            key_rows.astype(jnp.float32),
            precision=lax.Precision.HIGHEST,
        )
        * score_scale
    )
    live_mask = is_live[..., None, :]
    scores = jnp.where(live_mask, scores, -1e30)
    run_max = jnp.max(scores, axis=-1)
    weights = jnp.exp(scores - run_max[..., None]) * live_mask
    run_sum = jnp.sum(weights, axis=-1)
    run_out = jnp.einsum(
        "...ql,...ld->...qd",
        weights,
        value_rows.astype(jnp.float32),
        precision=lax.Precision.HIGHEST,
    )
    return (run_max, run_sum, run_out)


def combine(earlier, later):
    joint_max = jnp.maximum(earlier[0], later[0])
    scale_early = jnp.exp(earlier[0] - joint_max)
    scale_late = jnp.exp(later[0] - joint_max)
    return (
        joint_max,
        earlier[1] * scale_early + later[1] * scale_late,
        earlier[2] * scale_early[..., None] + later[2] * scale_late[..., None],
    )


def on_device(
    cache_keys,
    cache_values,
    sketch_matrix,
    queries,
    fresh_keys,
    fresh_values,
    chosen,
    shard_counts,
    outliers,
):
    seq_len, feature_width = cache_keys.shape
    devices = lax.axis_size("seq")
    myself = lax.axis_index("seq")
    length = seq_len * devices
    steps = queries.shape[0]
    group_size = QH // KVH
    per_device = QH // devices
    contract = (((0,), (0,)), ((), ()))
    gram_share = (
        lax.psum_scatter(
            lax.dot_general(cache_keys, cache_keys, contract, preferred_element_type=jnp.float32),
            "seq",
            scatter_dimension=0,
            tiled=True,
        )
        / length
    )
    sketch_share = jnp.dot(gram_share, sketch_matrix, precision=lax.Precision.HIGHEST)
    sketch = lax.all_gather(sketch_share, "seq", axis=0, tiled=True)
    key_basis = make_basis(sketch)
    rank_width = key_basis.shape[1]
    key_factor = jnp.dot(cache_keys, key_basis, preferred_element_type=jnp.float32)
    spans_dev = seq_len // SPAN
    most_slots = 3 * chosen.shape[2] // devices
    preceding = jnp.cumsum(shard_counts, axis=2) - shard_counts
    list_start = lax.dynamic_index_in_dim(preceding, myself, 2, keepdims=False)
    own_count = lax.dynamic_index_in_dim(shard_counts, myself, 2, keepdims=False)
    padded_list = jnp.concatenate([chosen, jnp.zeros((steps, KVH, most_slots), jnp.int32)], axis=2)
    slot_ids = jnp.arange(most_slots, dtype=jnp.int32)
    picked = jnp.take_along_axis(padded_list, list_start[..., None] + slot_ids, axis=2)
    is_live = slot_ids < own_count[..., None]
    shard_base = myself * spans_dev
    local_span = jnp.clip(picked - shard_base, 0, spans_dev - 1)
    factor_spans = key_factor.reshape(spans_dev, SPAN, rank_width)[local_span]
    basis_heads = key_basis.reshape(KVH, HD, rank_width).astype(jnp.float32)
    rebuilt = jnp.einsum(
        "tgmcr,gdr->tgmcd", factor_spans, basis_heads, precision=lax.Precision.HIGHEST
    )
    token_pos = (local_span + shard_base)[..., None] * SPAN + jnp.arange(SPAN, dtype=jnp.int32)
    sel_keys = rotate(rebuilt, token_pos).astype(jnp.bfloat16)
    value_blocks = cache_values.reshape(spans_dev, SPAN, KVH, HD)
    head_ids = jnp.arange(KVH, dtype=jnp.int32)
    sel_values = value_blocks[local_span, :, head_ids[None, :, None], :]
    outlier_here = outliers // spans_dev == myself
    outlier_order = jnp.cumsum(outlier_here.astype(jnp.int32)) - 1
    slot_match = outlier_here[None, :] & (
        outlier_order[None, :] == jnp.arange(OMOST, dtype=jnp.int32)[:, None]
    )
    outlier_local = jnp.sum(jnp.where(slot_match, outliers[None, :] - shard_base, 0), axis=1)
    outlier_live = jnp.any(slot_match, axis=1)
    key_blocks = cache_keys.reshape(spans_dev, SPAN, KVH, HD)
    out_keys = key_blocks[outlier_local[None, :], :, head_ids[:, None], :]
    out_pos = (outlier_local + shard_base)[:, None] * SPAN + jnp.arange(SPAN, dtype=jnp.int32)
    out_keys = rotate(out_keys.astype(jnp.float32), out_pos).astype(jnp.bfloat16)
    out_values = value_blocks[outlier_local[None, :], :, head_ids[:, None], :]
    slot_total = most_slots + OMOST
    slot_keys = jnp.concatenate(
        [sel_keys, jnp.broadcast_to(out_keys[None], (steps, KVH, OMOST, SPAN, HD))], axis=2
    )
    slot_values = jnp.concatenate(
        [sel_values, jnp.broadcast_to(out_values[None], (steps, KVH, OMOST, SPAN, HD))], axis=2
    )
    slot_live = jnp.concatenate(
        [is_live, jnp.broadcast_to(outlier_live[None, None], (steps, KVH, OMOST))], axis=2
    )
    step_pos = length + jnp.arange(steps, dtype=jnp.int32)
    query_rows = rotate(queries.reshape(steps, QH, HD).astype(jnp.float32), step_pos[:, None])
    own_queries = lax.dynamic_slice_in_dim(query_rows, myself * per_device, per_device, 1)
    grouped = query_rows.reshape(steps, KVH, group_size, HD)
    flat_keys = slot_keys.reshape(steps, KVH, slot_total * SPAN, HD)
    flat_values = slot_values.reshape(steps, KVH, slot_total * SPAN, HD)
    token_live = jnp.repeat(slot_live, SPAN, axis=2)
    local_stats = softmax_part(grouped, flat_keys, flat_values, token_live)
    merged = merged_2(local_stats, "seq", combine)
    run_max = lax.dynamic_slice_in_dim(
        merged[0].reshape(steps, QH), myself * per_device, per_device, 1
    )
    run_sum = lax.dynamic_slice_in_dim(
        merged[1].reshape(steps, QH), myself * per_device, per_device, 1
    )
    run_out = lax.dynamic_slice_in_dim(
        merged[2].reshape(steps, QH, HD), myself * per_device, per_device, 1
    )
    own_head = myself * per_device // group_size
    new_keys = lax.dynamic_index_in_dim(
        fresh_keys.reshape(steps, KVH, HD), own_head, 1, keepdims=False
    )
    new_keys = rotate(new_keys.astype(jnp.float32), step_pos).astype(jnp.bfloat16)
    new_values = lax.dynamic_index_in_dim(
        fresh_values.reshape(steps, KVH, HD), own_head, 1, keepdims=False
    )
    score_scale = 1.0 / jnp.sqrt(jnp.float32(HD))
    new_scores = (
        jnp.einsum(
            "thd,sd->ths",
            own_queries,
            new_keys.astype(jnp.float32),
            precision=lax.Precision.HIGHEST,
        )
        * score_scale
    )
    causal = jnp.arange(steps)[None, :] <= jnp.arange(steps)[:, None]
    new_scores = jnp.where(causal[:, None, :], new_scores, -1e30)
    joint_max = jnp.maximum(run_max, jnp.max(new_scores, axis=-1))
    old_scale = jnp.exp(run_max - joint_max)
    new_weights = jnp.exp(new_scores - joint_max[..., None]) * causal[:, None, :]
    summed = run_out * old_scale[..., None] + jnp.einsum(
        "ths,sd->thd", new_weights, new_values.astype(jnp.float32), precision=lax.Precision.HIGHEST
    )
    totals = run_sum * old_scale + jnp.sum(new_weights, axis=-1)
    attended = (summed / totals[..., None]).reshape(steps, per_device * HD).astype(jnp.bfloat16)
    return (attended, key_factor)


def solution(mesh):
    in_specs = (
        P(("groups", "seq"), None),
        P(("groups", "seq"), None),
        P(),
        P("groups", None),
        P("groups", None),
        P("groups", None),
        P("groups", None, None),
        P("groups", None, None),
        P("groups"),
    )
    out_specs = (P("groups", "seq"), P(("groups", "seq"), None))
    return jax.shard_map(
        on_device, mesh=mesh, in_specs=in_specs, out_specs=out_specs, check_vma=False
    )
```

profile of v0, /device:TPU:0, one launch (start us, length us, event | category | flops | bytes accessed | tf_op | source)
XLA Modules:
  0.0 298.8 jit_solution(4955914066819933756)
XLA Ops:
  7.2 15.1 %fusion.89 = f32[1024,1024]{1,0:T(8,128)} fusion(bf16[4096,1024]{1,0:T(8,128)(2,1)} %param.11), kind=kOutput, calls=%fused_computation.175 | convolution fusion | flops 8589934592 | bytes 12582912 | tf_op jit(solution)/shard_map/dot_general | solution.py:102
  23.4 9.4 %gather_fusion.4 = s32[1152]{0:T(1024)S(1)} fusion(s32[3,8,304]{2,1,0:T(8,128)S(1)} %concatenate.47, s32[1152]{0:T(1024)S(1)} %reshape.400), kind=kCustom, calls=%fused_computation.4 | custom fusion | bytes 23040 | tf_op jit(solution)/shard_map/jit(take_along_axis)/gather | solution.py:121
  33.8 4.5 %gather_fusion.1 = bf16[32,8,128]{2,1,0:T(8,128)(2,1)S(1)} fusion(bf16[512,8,8,128]{3,1,2,0:T(8,128)(2,1)} %bitcast.140, s32[32]{0:T(128)S(1)} %reshape.382), kind=kCustom, calls=%fused_computation.1 | custom fusion | bytes 131328 | tf_op jit(solution)/shard_map/gather | solution.py:143
  39.7 5.1 %gather_fusion.3 = bf16[32,8,128]{2,1,0:T(8,128)(2,1)} fusion(bf16[512,8,8,128]{3,1,2,0:T(8,128)(2,1)} %bitcast.145, s32[32]{0:T(128)S(1)} %reshape.382), kind=kCustom, calls=%fused_computation.3 | custom fusion | bytes 131328 | tf_op jit(solution)/shard_map/gather | solution.py:146
  44.8 14.9 %gather_fusion.2 = bf16[1152,8,128]{2,1,0:T(8,128)(2,1)} fusion(bf16[512,8,8,128]{3,1,2,0:T(8,128)(2,1)} %bitcast.146, s32[1152]{0:T(1024)S(1)} %reshape.388), kind=kCustom, calls=%fused_computation.2 | custom fusion | bytes 4727808 | tf_op jit(solution)/shard_map/gather | solution.py:134
  63.1 35.0 %reduce-scatter.2.cloned.1.call-done = f32[64,1024]{1,0:T(8,128)} async-done(((f32[1024,1024]{1,0:T(8,128)}), f32[64,1024]{1,0:T(8,128)}) %reduce-scatter.2.cloned.1.call-update) | async-done | bytes 262160 | tf_op jit(solution)/shard_map/reduce_scatter | solution.py:101
  98.1 1.7 fusion.36
  99.8 22.3 %all_gather.21 = f32[1024,160]{1,0:T(8,128)S(1)} all-gather(f32[64,160]{1,0:T(8,128)S(1)} %fusion.36), channel_id=1, replica_groups=mesh['groups'=2,'seq'=16] {'seq'}, dimensions={0}, use_global_device_ids=true | all-gather | bytes 696320 | tf_op jit(solution)/shard_map/all_gather | solution.py:110
  122.1 1.9 fusion.90
  124.1 11.7 %cholesky.51 = f32[128,128]{1,0:T(8,128)S(1)} custom-call(f32[128,128]{1,0:T(8,128)S(1)} %cholesky.124), custom_call_target="Cholesky" | custom-call | tf_op jit(solution)/shard_map/jit(cholesky)/cholesky | solution.py:40
  135.9 9.8 %custom-call.14 = f32[1,128,128]{1,2,0:T(8,128)S(1)} custom-call(f32[1,128,128]{2,1,0:T(8,128)S(1)} %get-tuple-element.236), custom_call_target="InvertDiagBlocksLowerTriangular" | custom-call | tf_op jit(solution)/shard_map/jit(cholesky)/cholesky | solution.py:40
  146.0 2.9 cholesky.110
  151.7 19.9 %custom-call.15 = f32[2,128,128]{1,2,0:T(8,128)S(1)} custom-call(f32[2,128,128]{2,1,0:T(8,128)S(1)} %pad_maximum_fusion.3), custom_call_target="InvertDiagBlocksLowerTriangular" | custom-call | tf_op jit(solution)/shard_map/triangular_solve | solution.py:41
  173.9 6.3 %convolution_bitcast_fusion = f32[4096,160]{0,1:T(8,128)S(1)} fusion(bf16[4096,1024]{1,0:T(8,128)(2,1)} %param.11, bf16[32,1024]{1,0:T(8,128)(2,1)S(1)} %convolution_convert_fusion, bf16[128,1024]{1,0:T(8,128)(2,1)S(1)} %get-tuple-element.249), kind=kOutput, calls=%fused_computation.21 | convolution fusion | flops 1342832640 | bytes 11337728 | tf_op jit(solution)/shard_map/dot_general | solution.py:113
  181.0 3.3 %copy.41 = f32[4096,160]{1,0:T(8,128)} copy(f32[4096,160]{0,1:T(8,128)S(1)} %convolution_bitcast_fusion) | data formatting | bytes 5242880 | tf_op jit(solution)/shard_map/dot_general | solution.py:113
  184.4 1.8 copy.55
  186.1 10.0 %gather_fusion = f32[1152,8,160]{2,1,0:T(8,128)} fusion(f32[512,8,160]{2,1,0:T(8,128)} %bitcast.136, s32[2048]{0:T(1024)} %pad_clamp_fusion), kind=kCustom, calls=%fused_computation | custom fusion | bytes 11801088 | tf_op jit(solution)/shard_map/gather | solution.py:125
  196.1 11.9 %fusion.19 = f32[3,8,48,8,128]{4,2,3,0,1:T(8,128)S(1)} fusion(f32[3,8,48,8,160]{4,3,2,1,0:T(8,128)} %bitcast.137, bf16[8,128,160,1,1]{1,0,2,4,3:T(8,128)(2,1)} %bitcast.143), kind=kOutput, calls=%fused_computation.34 | convolution fusion | flops 2264924160 | bytes 10944512 | tf_op jit(solution)/shard_map/tgmcr,gdr->tgmcd/dot_general | solution.py:127
  208.1 19.4 %fusion.10 = (bf16[3,8,48,8,64]{4,2,3,0,1:T(8,128)(2,1)S(1)}, bf16[3,8,48,8,64]{4,2,3,0,1:T(8,128)(2,1)S(1)}) fusion(f32[3,8,48,8,128]{4,2,3,0,1:T(8,128)S(1)} %fusion.19, f32[64]{0:T(128)S(1)} %multiply_exponential_fusion, f32[3,8,48,8]{2,3,0,1:T(8,128)S(1)} %copy-done.3), kind=kLoop, calls=%fused_computation.23 | loop fusion | flops 5308416 | bytes 7115008 | tf_op jit(solution)/shard_map/convert.11
  229.1 3.0 fusion.87
  232.1 2.2 fusion.13
  234.9 19.2 %all-gather.1 = f32[48,8,8]{2,1,0:T(8,128)S(1)} all-gather(f32[3,8,8]{2,1,0:T(8,128)S(1)} %fusion.35), channel_id=3, replica_groups=mesh['groups'=2,'seq'=16] {'seq'}, dimensions={0}, use_global_device_ids=true | all-gather | bytes 13056 | tf_op jit(solution)/shard_map/all_gather | solution.py:14
  254.1 18.4 %all-gather = f32[48,8,8]{2,1,0:T(8,128)S(1)} all-gather(f32[3,8,8]{2,1,0:T(8,128)S(1)} %get-tuple-element.251), channel_id=2, replica_groups=mesh['groups'=2,'seq'=16] {'seq'}, dimensions={0}, use_global_device_ids=true | all-gather | bytes 13056 | tf_op jit(solution)/shard_map/all_gather | solution.py:14
  273.4 16.3 %while.21 = (s32[]{:T(128)}, f32[3,8,8]{2,1,0:T(8,128)S(1)}, f32[3,8,8]{2,1,0:T(8,128)S(1)}, f32[3,8,8,128]{3,2,1,0:T(8,128)S(1)}, f32[16,3,8,8]{3,2,1,0:T(8,128...) while((s32[]{:T(128)}, f32[3,8,8]{2,1,0:T(8,128)S(1)}, ...), condition=%wide.region_12.13_spmd, body=%wide.region_11.12_spmd.sunk | while | flops 74885 | bytes 302743 | solution.py:20
  (139 shorter events, 32.5 us)
Async XLA Ops:
  7.2 90.9 %copy-start = (f32[1024,160]{0,1:T(8,128)S(1)}, f32[1024,160]{0,1:T(8,128)}, u32[]{:S(2)}) copy-start(f32[1024,160]{0,1:T(8,128)} %param.13) | copy-start | bytes 1966084
  7.2 15.3 %copy-start.7 = (s32[3,8,16]{2,1,0:T(8,128)S(1)}, s32[3,8,16]{2,1,0:T(8,128)}, u32[]{:S(2)}) copy-start(s32[3,8,16]{2,1,0:T(8,128)} %param.18) | copy-start | bytes 4612
  7.2 16.2 %copy-start.8 = (s32[3,8,256]{2,1,0:T(8,128)S(1)}, s32[3,8,256]{2,1,0:T(8,128)}, u32[]{:S(2)}) copy-start(s32[3,8,256]{2,1,0:T(8,128)} %param.17) | copy-start | bytes 73732
  7.2 90.9 %reduce-scatter.2.cloned.1.call-start = ((), (), s32[]{:S(2)}) async-start(), calls=%async_computation.1 | async-start | bytes 4456448 | tf_op jit(solution)/shard_map/reduce_scatter | solution.py:101
  22.4 250.1 %all-gather.5.cloned.1.call-start = ((), (), s32[]{:S(2)}) async-start(), calls=%async_computation.2 | async-start | bytes 1671168 | tf_op jit(solution)/shard_map/all_gather | solution.py:14
  23.4 9.9 %copy-start.11 = (s32[32]{0:T(128)S(1)}, s32[32]{0:T(128)}, u32[]{:S(2)}) copy-start(s32[32]{0:T(128)} %param.19) | copy-start | bytes 388
  23.4 15.4 %copy-start.6 = (bf16[3,8192]{1,0:T(4,128)(2,1)S(1)}, bf16[3,8192]{1,0:T(4,128)(2,1)}, u32[]{:S(2)}) copy-start(bf16[3,8192]{1,0:T(4,128)(2,1)} %param.14) | copy-start | bytes 147460
  180.2 15.9 %copy-start.1 = (f32[4096,160]{0,1:T(8,128)}, f32[4096,160]{0,1:T(8,128)S(1)}, u32[]{:S(2)}) copy-start(f32[4096,160]{0,1:T(8,128)S(1)} %convolution_bitcast_fusion) | copy-start | bytes 7864324
  196.1 12.0 %copy-start.3 = (f32[3,8,48,8]{2,3,0,1:T(8,128)S(1)}, f32[3,8,48,8]{2,3,0,1:T(8,128)}, u32[]{:S(2)}) copy-start(f32[3,8,48,8]{2,3,0,1:T(8,128)} %add_convert_fusion.1) | copy-start | bytes 110596
  227.6 4.5 %copy-start.4 = (bf16[32,8,128]{2,1,0:T(8,128)(2,1)S(1)}, bf16[32,8,128]{2,1,0:T(8,128)(2,1)}, u32[]{:S(2)}) copy-start(bf16[32,8,128]{2,1,0:T(8,128)(2,1)} %gather_fusion.3) | copy-start | bytes 196612
  227.6 4.5 %copy-start.2 = (bf16[1152,8,128]{2,1,0:T(8,128)(2,1)S(1)}, bf16[1152,8,128]{2,1,0:T(8,128)(2,1)}, u32[]{:S(2)}) copy-start(bf16[1152,8,128]{2,1,0:T(8,128)(2,1)} %gather_fusion.2) | copy-start | bytes 7077892
  227.6 4.5 %copy-start.5 = (f32[3,8,416]{2,1,0:T(8,128)S(1)}, f32[3,8,416]{2,1,0:T(8,128)}, u32[]{:S(2)}) copy-start(f32[3,8,416]{2,1,0:T(8,128)} %convert_element_type.103) | copy-start | bytes 119812
  229.0 5.3 %copy-start.9 = (bf16[3,64]{1,0:T(4,128)(2,1)S(1)}, bf16[3,64]{1,0:T(4,128)(2,1)}, u32[]{:S(2)}) copy-start(bf16[3,64]{1,0:T(4,128)(2,1)} %get-tuple-element.239) | copy-start | bytes 1156
  229.1 5.3 %copy-start.10 = (bf16[3,64]{1,0:T(4,128)(2,1)S(1)}, bf16[3,64]{1,0:T(4,128)(2,1)}, u32[]{:S(2)}) copy-start(bf16[3,64]{1,0:T(4,128)(2,1)} %get-tuple-element.240) | copy-start | bytes 1156
Sparse Core Ops, SparseCore 0:
  22.5 75.5 reduce-scatter.1
  234.4 37.8 all-gather.4
where the time goes:
time: 303 us; the launch traced here: 299 us
  other arithmetic  89.2 us (29%)
  blocking collectives  59.9 us (20%)
  local copies, waits for them, and re-layouts  52.1 us (17%)
  matrix products  46 us (15%)
  waiting for transfers between devices  35 us (12%)
  between operations  16.1 us (5%)
    all_gather x2, blocking collectives, merged_2(): everything = jax.tree.map(lambda part: lax.all_gather(part, axis), x)  37.6 us
    reduce_scatter x1, waiting for transfers between devices, on_device(): lax.psum_scatter(lax.dot_general(cache_keys, cache_keys, contract, prefer...  35 us
    another operation x7, other arithmetic, make_basis(): lower = jnp.linalg.cholesky(small_gram)  25.8 us
    all_gather x1, blocking collectives, on_device(): sketch = lax.all_gather(sketch_share, 'seq', axis=0, tiled=True)  22.3 us
    another operation x5, other arithmetic  20.3 us
    another operation x6, other arithmetic, make_basis(): lax.linalg.triangular_solve(lower, sketch.T, left_side=True, lower=True)  20 us
    add x15, other arithmetic, combine(): earlier[2] * scale_early[..., None] + later[2] * scale_late[..., None]  15.6 us
    dot_general x1, matrix products, on_device(): lax.dot_general(cache_keys, cache_keys, contract, preferred_element_type=...  15.1 us
  transfers between devices with their start and end apart: 2, of which 1 were waited for; matrix products, arithmetic and copies ran while one was open for 14% of the time, Pallas kernels for 0%

commit v1 on v0

--- a/solution.py
+++ b/solution.py
@@ -107,7 +107,14 @@
         / length
     )
     sketch_share = jnp.dot(gram_share, sketch_matrix, precision=lax.Precision.HIGHEST)
-    sketch = lax.all_gather(sketch_share, "seq", axis=0, tiled=True)
+    ways, here, step_2 = (lax.axis_size("seq"), lax.axis_index("seq"), sketch_share.shape[0])
+    line, have = (sketch_share, 1)
+    while have < ways:
+        line = jnp.concatenate(
+            [line, lax.ppermute(line, "seq", [(d, (d - have) % ways) for d in range(ways)])], axis=0
+        )
+        have = 2 * have
+    sketch = jnp.roll(line, here * step_2, axis=0)
     key_basis = make_basis(sketch)
     rank_width = key_basis.shape[1]
     key_factor = jnp.dot(cache_keys, key_basis, preferred_element_type=jnp.float32)

time: 303 us -> 347 us (1.15)
  waiting for transfers between devices: 35 us -> 87.3 us
  blocking collectives: 59.9 us -> 40 us
  local copies, waits for them, and re-layouts: 52.1 us -> 56.5 us
  starting transfers between devices: 0.08 us -> 4.45 us
    ppermute x0 -> x4, waiting for transfers between devices: none -> 31.1 us  [on_device(): lax.ppermute(line, 'seq', [(d, (d - have) % ways) for d in range(ways)])]
    all_gather x1 -> x0, blocking collectives: 22.3 us -> none  [on_device(): sketch = lax.all_gather(sketch_share, 'seq', axis=0, tiled=True)]
    reduce_scatter x1, waiting for transfers between devices: 35 us -> 56.2 us  [on_device(): lax.psum_scatter(lax.dot_general(cache_keys, cache_keys, contract, prefer...]
    ppermute x0 -> x4, starting transfers between devices: none -> 4.37 us  [on_device(): lax.ppermute(line, 'seq', [(d, (d - have) % ways) for d in range(ways)])]
  transfers between devices with their start and end apart: 2 -> 6, of which waited for: 1 -> 4; matrix products, arithmetic and copies ran while one was open for 14% -> 13% of each run, Pallas kernels for 0% -> 0%
where the time goes in v1:
time: 347 us; the launch traced here: 341 us
  other arithmetic  91.2 us (26%)
  waiting for transfers between devices  87.3 us (25%)
  local copies, waits for them, and re-layouts  56.5 us (16%)
  matrix products  45.2 us (13%)
  blocking collectives  40 us (12%)
  between operations  16.2 us (5%)
  starting transfers between devices  4.45 us (1%)
    reduce_scatter x1, waiting for transfers between devices, on_device(): lax.psum_scatter(lax.dot_general(cache_keys, cache_keys, contract, prefer...  56.2 us
    all_gather x2, blocking collectives, merged_2(): everything = jax.tree.map(lambda part: lax.all_gather(part, axis), x)  40 us
    ppermute x4, waiting for transfers between devices, on_device(): lax.ppermute(line, 'seq', [(d, (d - have) % ways) for d in range(ways)])  31.1 us
    another operation x7, other arithmetic, make_basis(): lower = jnp.linalg.cholesky(small_gram)  25.8 us
    another operation x6, other arithmetic, make_basis(): lax.linalg.triangular_solve(lower, sketch.T, left_side=True, lower=True)  21.3 us
    another operation x5, other arithmetic  20.3 us
    add x15, other arithmetic, combine(): earlier[2] * scale_early[..., None] + later[2] * scale_late[..., None]  15.6 us
    dot_general x1, matrix products, on_device(): lax.dot_general(cache_keys, cache_keys, contract, preferred_element_type=...  15.1 us
  transfers between devices with their start and end apart: 6, of which 4 were waited for; matrix products, arithmetic and copies ran while one was open for 13% of the time, Pallas kernels for 0%

profile of v1, /device:TPU:0, one launch (start us, length us, event | category | flops | bytes accessed | tf_op | source)
XLA Modules:
  0.0 341.3 jit_solution(9279495782561762764)
XLA Ops:
  7.2 15.1 %fusion.93 = f32[1024,1024]{1,0:T(8,128)} fusion(bf16[4096,1024]{1,0:T(8,128)(2,1)} %param.11), kind=kOutput, calls=%fused_computation.193 | convolution fusion | flops 8589934592 | bytes 12582912 | tf_op jit(solution)/shard_map/dot_general | solution.py:102
  24.0 9.0 %gather_fusion.4 = s32[1152]{0:T(1024)S(1)} fusion(s32[3,8,304]{2,1,0:T(8,128)S(1)} %concatenate.69, s32[1152]{0:T(1024)S(1)} %reshape.400), kind=kCustom, calls=%fused_computation.4 | custom fusion | bytes 23040 | tf_op jit(solution)/shard_map/jit(take_along_axis)/gather | solution.py:128
  33.7 4.5 %gather_fusion.1 = bf16[32,8,128]{2,1,0:T(8,128)(2,1)S(1)} fusion(bf16[512,8,8,128]{3,1,2,0:T(8,128)(2,1)} %bitcast.136, s32[32]{0:T(128)S(1)} %reshape.382), kind=kCustom, calls=%fused_computation.1 | custom fusion | bytes 131328 | tf_op jit(solution)/shard_map/gather | solution.py:150
  41.8 56.2 %reduce-scatter.2.cloned.1.call-done = f32[64,1024]{1,0:T(8,128)} async-done(((f32[1024,1024]{1,0:T(8,128)}), f32[64,1024]{1,0:T(8,128)}) %reduce-scatter.2.cloned.1.call-update) | async-done | bytes 262160 | tf_op jit(solution)/shard_map/reduce_scatter | solution.py:101
  101.7 2.0 collective-permute-start.1
  104.4 3.5 %collective-permute-done.1 = f32[128,160]{1,0:T(8,128)S(1)} collective-permute-done((f32[128,160]{1,0:T(8,128)S(1)}, f32[128,160]{1,0:T(8,128)S(1)}, u32[]{:S(2)}, u32[]{:S(2)}) %collective-permute-start.1) | collective-permute-done | bytes 81952 | tf_op jit(solution)/shard_map/ppermute | solution.py:114
  114.7 4.6 %gather_fusion.3 = bf16[32,8,128]{2,1,0:T(8,128)(2,1)} fusion(bf16[512,8,8,128]{3,1,2,0:T(8,128)(2,1)} %bitcast.141, s32[32]{0:T(128)S(1)} %reshape.382), kind=kCustom, calls=%fused_computation.3 | custom fusion | bytes 131328 | tf_op jit(solution)/shard_map/gather | solution.py:153
  119.4 14.9 %gather_fusion.2 = bf16[1152,8,128]{2,1,0:T(8,128)(2,1)} fusion(bf16[512,8,8,128]{3,1,2,0:T(8,128)(2,1)} %bitcast.142, s32[1152]{0:T(1024)S(1)} %reshape.388), kind=kCustom, calls=%fused_computation.2 | custom fusion | bytes 4727808 | tf_op jit(solution)/shard_map/gather | solution.py:141
  135.9 25.8 %collective-permute-done.3 = f32[512,160]{1,0:T(8,128)S(1)} collective-permute-done((f32[512,160]{1,0:T(8,128)S(1)}, f32[512,160]{1,0:T(8,128)S(1)}, u32[]{:S(2)}, u32[]{:S(2)}) %collective-permute-start.3) | collective-permute-done | bytes 327712 | tf_op jit(solution)/shard_map/ppermute | solution.py:114
  163.2 2.1 fusion.32
  166.7 11.7 %cholesky.51 = f32[128,128]{1,0:T(8,128)S(1)} custom-call(f32[128,128]{1,0:T(8,128)S(1)} %cholesky.124), custom_call_target="Cholesky" | custom-call | tf_op jit(solution)/shard_map/jit(cholesky)/cholesky | solution.py:40
  178.5 9.8 %custom-call.14 = f32[1,128,128]{1,2,0:T(8,128)S(1)} custom-call(f32[1,128,128]{2,1,0:T(8,128)S(1)} %get-tuple-element.236), custom_call_target="InvertDiagBlocksLowerTriangular" | custom-call | tf_op jit(solution)/shard_map/jit(cholesky)/cholesky | solution.py:40
  188.6 2.9 cholesky.110
  194.4 19.9 %custom-call.15 = f32[2,128,128]{1,2,0:T(8,128)S(1)} custom-call(f32[2,128,128]{2,1,0:T(8,128)S(1)} %pad_maximum_fusion.6), custom_call_target="InvertDiagBlocksLowerTriangular" | custom-call | tf_op jit(solution)/shard_map/triangular_solve | solution.py:41
  216.6 6.3 %convolution_bitcast_fusion = f32[4096,160]{0,1:T(8,128)S(1)} fusion(bf16[4096,1024]{1,0:T(8,128)(2,1)} %param.11, bf16[32,1024]{1,0:T(8,128)(2,1)S(1)} %convolution_convert_fusion, bf16[128,1024]{1,0:T(8,128)(2,1)S(1)} %get-tuple-element.251), kind=kOutput, calls=%fused_computation.21 | convolution fusion | flops 1342832640 | bytes 11337728 | tf_op jit(solution)/shard_map/dot_general | solution.py:120
  223.8 3.3 copy.41
  227.1 9.9 %gather_fusion = f32[1152,8,160]{2,1,0:T(8,128)} fusion(f32[512,8,160]{2,1,0:T(8,128)} %bitcast.134, s32[2048]{0:T(1024)S(1)} %copy-done.12), kind=kCustom, calls=%fused_computation | custom fusion | bytes 11801088 | tf_op jit(solution)/shard_map/gather | solution.py:132
  237.0 11.0 %fusion.19 = f32[3,8,48,8,128]{4,2,3,0,1:T(8,128)S(1)} fusion(f32[3,8,48,8,160]{4,3,2,1,0:T(8,128)} %bitcast.135, bf16[8,128,160,1,1]{1,0,2,4,3:T(8,128)(2,1)S(1)} %bitcast.139), kind=kOutput, calls=%fused_computation.34 | convolution fusion | flops 2264924160 | bytes 10944512 | tf_op jit(solution)/shard_map/tgmcr,gdr->tgmcd/dot_general | solution.py:134
  248.1 19.4 %fusion.10 = (bf16[3,8,48,8,64]{4,2,3,0,1:T(8,128)(2,1)S(1)}, bf16[3,8,48,8,64]{4,2,3,0,1:T(8,128)(2,1)S(1)}) fusion(f32[3,8,48,8,128]{4,2,3,0,1:T(8,128)S(1)} %fusion.19, f32[64]{0:T(128)S(1)} %copy-done.16, f32[3,8,48,8]{2,3,0,1:T(8,128)S(1)} %copy-done.5), kind=kLoop, calls=%fused_computation.23 | loop fusion | flops 5308416 | bytes 7115008 | tf_op jit(solution)/shard_map/convert.11
  269.1 3.0 fusion.91
  272.2 2.2 fusion.13
  274.9 21.6 %all-gather.1 = f32[48,8,8]{2,1,0:T(8,128)S(1)} all-gather(f32[3,8,8]{2,1,0:T(8,128)S(1)} %fusion.37), channel_id=3, replica_groups=mesh['groups'=2,'seq'=16] {'seq'}, dimensions={0}, use_global_device_ids=true | all-gather | bytes 13056 | tf_op jit(solution)/shard_map/all_gather | solution.py:14
  296.6 18.4 %all-gather = f32[48,8,8]{2,1,0:T(8,128)S(1)} all-gather(f32[3,8,8]{2,1,0:T(8,128)S(1)} %get-tuple-element.253), channel_id=2, replica_groups=mesh['groups'=2,'seq'=16] {'seq'}, dimensions={0}, use_global_device_ids=true | all-gather | bytes 13056 | tf_op jit(solution)/shard_map/all_gather | solution.py:14
  315.9 16.3 %while.21 = (s32[]{:T(128)}, f32[3,8,8]{2,1,0:T(8,128)S(1)}, f32[3,8,8]{2,1,0:T(8,128)S(1)}, f32[3,8,8,128]{3,2,1,0:T(8,128)S(1)}, f32[16,3,8,8]{3,2,1,0:T(8,128...) while((s32[]{:T(128)}, f32[3,8,8]{2,1,0:T(8,128)S(1)}, ...), condition=%wide.region_12.13_spmd, body=%wide.region_11.12_spmd.sunk | while | flops 74885 | bytes 302743 | solution.py:20
  (175 shorter events, 47.5 us)
Async XLA Ops:
  7.2 90.8 %copy-start = (f32[1024,160]{0,1:T(8,128)S(1)}, f32[1024,160]{0,1:T(8,128)}, u32[]{:S(2)}) copy-start(f32[1024,160]{0,1:T(8,128)} %param.13) | copy-start | bytes 1966084
  7.2 90.8 %reduce-scatter.2.cloned.1.call-start = ((), (), s32[]{:S(2)}) async-start(), calls=%async_computation.1 | async-start | bytes 4456448 | tf_op jit(solution)/shard_map/reduce_scatter | solution.py:101
  22.3 1.6 copy-start.14
  22.4 292.6 %all-gather.5.cloned.1.call-start = ((), (), s32[]{:S(2)}) async-start(), calls=%async_computation.2 | async-start | bytes 1671168 | tf_op jit(solution)/shard_map/all_gather | solution.py:14
  24.0 9.3 %copy-start.19 = (s32[32]{0:T(128)S(1)}, s32[32]{0:T(128)}, u32[]{:S(2)}) copy-start(s32[32]{0:T(128)} %param.19) | copy-start | bytes 388
  24.0 14.2 %copy-start.11 = (bf16[3,8192]{1,0:T(4,128)(2,1)S(1)}, bf16[3,8192]{1,0:T(4,128)(2,1)}, u32[]{:S(2)}) copy-start(bf16[3,8192]{1,0:T(4,128)(2,1)} %param.14) | copy-start | bytes 147460
  38.5 3.3 copy-start.15
  99.7 2.0 collective-permute-start
  101.7 6.1 %collective-permute-start.1 = (f32[128,160]{1,0:T(8,128)S(1)}, f32[128,160]{1,0:T(8,128)S(1)}, u32[]{:S(2)}, u32[]{:S(2)}) collective-permute-start(f32[128,160]{1,0:T(8,128)S(1)} %pad_maximum_fusion.5), channel_id=1, source_target_pairs={{0,14},{1,15},{2,0},{3,1},{4,2},{5,3},{6,4},{7,5},{8,6},{9,7},{10,... | collective-permute-start | bytes 245768 | tf_op jit(solution)/shard_map/ppermute | solution.py:114
  108.6 27.0 %collective-permute-start.2 = (f32[256,160]{1,0:T(8,128)}, f32[256,160]{1,0:T(8,128)S(1)}, u32[]{:S(2)}, u32[]{:S(2)}) collective-permute-start(f32[256,160]{1,0:T(8,128)} %pad_maximum_fusion.3), channel_id=1, source_target_pairs={{0,12},{1,13},{2,14},{3,15},{4,0},{5,1},{6,2},{7,3},{8,4},{9,5},{1... | collective-permute-start | bytes 491528 | tf_op jit(solution)/shard_map/ppermute | solution.py:114
  113.9 20.3 %copy-start.9 = (pred[3,8,416]{2,1,0:T(8,128)(4,1)}, pred[3,8,416]{2,1,0:T(8,128)(4,1)S(1)}, u32[]{:S(2)}) copy-start(pred[3,8,416]{2,1,0:T(8,128)(4,1)S(1)} %broadcast_in_dim.58) | copy-start | bytes 29956
  135.6 26.1 %collective-permute-start.3 = (f32[512,160]{1,0:T(8,128)S(1)}, f32[512,160]{1,0:T(8,128)S(1)}, u32[]{:S(2)}, u32[]{:S(2)}) collective-permute-start(f32[512,160]{1,0:T(8,128)S(1)} %pad_maximum_fusion.1), channel_id=1, source_target_pairs={{0,8},{1,9},{2,10},{3,11},{4,12},{5,13},{6,14},{7,15},{8,0},{9,1},... | collective-permute-start | bytes 983048 | tf_op jit(solution)/shard_map/ppermute | solution.py:114
  222.9 4.2 %copy-start.1 = (f32[4096,160]{0,1:T(8,128)}, f32[4096,160]{0,1:T(8,128)S(1)}, u32[]{:S(2)}) copy-start(f32[4096,160]{0,1:T(8,128)S(1)} %convolution_bitcast_fusion) | copy-start | bytes 7864324
  223.8 3.4 copy-start.12
  227.1 9.9 %copy-start.4 = (bf16[20,8,8,128]{3,2,1,0:T(8,128)(2,1)S(1)}, bf16[20,8,8,128]{3,2,1,0:T(8,128)(2,1)}, u32[]{:S(2)}) copy-start(bf16[20,8,8,128]{3,2,1,0:T(8,128)(2,1)} %copy.55) | copy-start | bytes 983044
  237.0 11.0 %copy-start.5 = (f32[3,8,48,8]{2,3,0,1:T(8,128)S(1)}, f32[3,8,48,8]{2,3,0,1:T(8,128)}, u32[]{:S(2)}) copy-start(f32[3,8,48,8]{2,3,0,1:T(8,128)} %add_convert_fusion.1) | copy-start | bytes 110596
  237.0 11.0 %copy-start.16 = (f32[64]{0:T(128)S(1)}, f32[64]{0:T(128)}, u32[]{:S(2)}) copy-start(f32[64]{0:T(128)} %copy-done.15) | copy-start | bytes 772
  248.1 19.5 %copy-start.7 = (bf16[8,4,8,128]{3,1,2,0:T(4,128)(2,1)S(1)}, bf16[8,4,8,128]{3,1,2,0:T(4,128)(2,1)}, u32[]{:S(2)}) copy-start(bf16[8,4,8,128]{3,1,2,0:T(4,128)(2,1)} %copy.45) | copy-start | bytes 196612
  267.6 1.5 copy-start.10
  269.1 3.0 copy-start.6
  269.1 3.1 copy-start.2
  269.1 3.1 copy-start.8
  272.1 2.3 copy-start.17
  272.1 2.3 copy-start.18
  (2 other events, 2.0 us)
Sparse Core Ops, SparseCore 0:
  22.5 75.4 reduce-scatter.1
  274.5 40.2 all-gather.4
